TPU v7x, 256 devices: a whole 4x4x8 slice. The times are simulated.
256 devices in a mesh: row: 16 (over z, core), col: 8 (over x_hi, y), feat: 2 (over x_lo).
Axes of the slice: x: 4 (x_hi: 2, x_lo: 2; x = x_hi * 2 + x_lo), y: 4, z: 8, core: 2. Of those that a mesh axis runs over, the one named last changes fastest.
Arguments:
- features: bfloat16 [65536, 256], P(('col', 'row'), 'feat'), may hold values from -6 to 6
- tile_rows: int32 [16, 8, 256], P('row', 'col'), may hold values from 0 to 31, as said below
- tile_cols: int32 [16, 8, 256], P('row', 'col'), may hold values from 0 to 63
- tile_count: int32 [16, 8], P('row', 'col'), may hold values from 64 to 256, as said below
- tile_values: bfloat16 [16, 8, 256, 128, 128], P('row', 'col'), may hold values from -0.21875 to 0.21875
- weights: bfloat16 [256, 256], replicated, may hold values from -0.375 to 0.375
- cotangent: bfloat16 [65536, 256], P(('row', 'col'), 'feat'), may hold values from -6 to 6
Outputs:
- activated: bfloat16 [65536, 256], P(('row', 'col'), 'feat')
- feature_grad: bfloat16 [65536, 256], P(('col', 'row'), 'feat')
- weight_grad: float32 [256, 256], P('feat')
Inputs may be any that keep to these rules, and one draw needn't show every extreme that they name: `tile_rows`: block rows of a cell, unevenly loaded. `tile_count`: some cell has all 256 slots live.
All inputs are finite; a program needn't handle non-finite values.
Results may differ from a plain program's by a relative error of at most 0.027.
Values may be sent and summed in bfloat16 or wider, within the bound.
A program may use at most 128 MiB of HBM per device.

v0:
```python
import jax
import jax.numpy as jnp
from jax import lax
from jax.sharding import PartitionSpec as P


def shards(features, tile_rows, tile_cols, tile_count, tile_values, weights, cotangent):
    width = tile_values.shape[-1]
    slots = tile_values.shape[2]
    local_tiles = tile_values[0, 0]
    block_rows = tile_rows[0, 0]
    block_cols = tile_cols[0, 0]
    live_mask = (jnp.arange(slots) < tile_count[0, 0]).astype(jnp.float32)
    n_rowdev = lax.axis_size("row")
    n_coldev = lax.axis_size("col")
    local_blocks = features.shape[0] // width
    feat_half = features.shape[1]
    feat_index = lax.axis_index("feat")
    row_blocks = local_blocks * n_coldev
    col_blocks = local_blocks * n_rowdev
    node_total = features.shape[0] * n_rowdev * n_coldev
    panel = lax.all_gather(features, "row", axis=0, tiled=True)
    gathered = panel.reshape(col_blocks, width, feat_half)[block_cols]
    products = jnp.einsum("tij,tjf->tif", local_tiles, gathered, preferred_element_type=jnp.float32)
    products = products * live_mask[:, None, None]
    partial_value = (
        jnp.zeros((row_blocks, width, feat_half), jnp.float32).at[block_rows].add(products)
    )
    summed = lax.psum_scatter(
        partial_value.reshape(row_blocks * width, feat_half).astype(jnp.bfloat16),
        "col",
        scatter_dimension=0,
        tiled=True,
    )
    weight_rows = lax.dynamic_slice_in_dim(weights, feat_index * feat_half, feat_half, 0)
    mix_term = jnp.dot(summed, weight_rows, preferred_element_type=jnp.float32)
    hidden = lax.psum_scatter(
        mix_term.astype(jnp.bfloat16), "feat", scatter_dimension=1, tiled=True
    ).astype(jnp.float32)
    negative = jnp.minimum(hidden, 0.0)
    activated = jnp.where(hidden > 0, hidden, jnp.expm1(negative)).astype(jnp.bfloat16)
    slope_factor = jnp.where(hidden > 0, 1.0, jnp.exp(negative))
    grad_out = (cotangent.astype(jnp.float32) * slope_factor).astype(jnp.bfloat16)
    grad_whole = lax.all_gather(grad_out, "feat", axis=1, tiled=True)
    weight_term = lax.dot_general(
        summed, grad_whole, (((0,), (0,)), ((), ())), preferred_element_type=jnp.float32
    )
    n_feat = lax.axis_size("feat")
    slots = jnp.zeros((n_feat,) + weight_term.shape, jnp.float32)
    slots = lax.dynamic_update_slice_in_dim(slots, weight_term[None], feat_index, 0)
    slots = lax.psum(slots, ("row", "col", "feat"))
    weight_grad = lax.dynamic_index_in_dim(slots, feat_index, 0, keepdims=False) * node_total ** (
        -0.5
    )
    spread = lax.dot_general(
        grad_whole, weight_rows, (((1,), (1,)), ((), ())), preferred_element_type=jnp.float32
    ).astype(jnp.bfloat16)
    spread_panel = lax.all_gather(spread, "col", axis=0, tiled=True)
    spread_blocks = spread_panel.reshape(row_blocks, width, feat_half)[block_rows]
    back_products = jnp.einsum(
        "tji,tjf->tif", local_tiles, spread_blocks, preferred_element_type=jnp.float32
    )
    back_products = back_products * live_mask[:, None, None]
    back_partial = (
        jnp.zeros((col_blocks, width, feat_half), jnp.float32).at[block_cols].add(back_products)
    )
    back_summed = lax.psum_scatter(
        back_partial.reshape(col_blocks * width, feat_half).astype(jnp.bfloat16),
        "row",
        scatter_dimension=0,
        tiled=True,
    )
    return (activated, back_summed, weight_grad)


def solution(mesh):
    return jax.shard_map(
        shards,
        mesh=mesh,
        in_specs=(
            P(("col", "row"), "feat"),
            P("row", "col", None),
            P("row", "col", None),
            P("row", "col"),
            P("row", "col", None, None, None),
            P(),
            P(("row", "col"), "feat"),
        ),
        out_specs=(P(("row", "col"), "feat"), P(("col", "row"), "feat"), P("feat", None)),
        check_vma=False,
    )
```

profile of v0, /device:TPU:2, one launch (start us, length us, event | category | flops | bytes accessed | tf_op | source)
XLA Modules:
  0.0 605.1 jit_solution(15216501221385841070)
XLA Ops:
  7.2 0.0 copy-start
  7.2 0.0 all-gather.3.cloned.1.call-start
  7.2 0.7 all-gather.3.cloned.1.call-update
  7.9 0.0 reduce-scatter.6.cloned.1.call-start
  8.6 0.7 compare_select_fusion
  9.3 43.2 %all-gather.3.cloned.1.call-done = bf16[8192,128]{1,0:T(8,128)(2,1)} async-done(((bf16[512,128]{1,0:T(8,128)(2,1)}), bf16[8192,128]{1,0:T(8,128)(2,1)}) %all-gather.3.cloned.1.call-update) | async-done | bytes 2097168 | tf_op jit(solution)/shard_map/all_gather | solution.py:22
  52.6 10.2 %gather_fusion = bf16[256,128,128]{2,1,0:T(8,128)(2,1)} fusion(bf16[64,128,128]{2,1,0:T(8,128)(2,1)} %bitcast.36, s32[1024]{0:T(1024)S(1)} %pad_clamp_fusion.1), kind=kCustom, calls=%fused_computation | custom fusion | bytes 16778240 | tf_op jit(solution)/shard_map/gather | solution.py:23
  62.8 13.0 %multiply_bitcast_fusion.1 = f32[256,128,128]{1,2,0:T(8,128)} fusion(bf16[256,128,128]{2,1,0:T(8,128)(2,1)} %gather_fusion, bf16[1,1,256,128,128]{4,3,2,1,0:T(8,128)(2,1)} %param.11, f32[256]{0:T(256)S(1)} %compare_convert_fusion), kind=kOutput, calls=%fused_computation.5 | convolution fusion | flops 1077936128 | bytes 33555456 | tf_op jit(solution)/shard_map/tij,tjf->tif/dot_general | solution.py:24
  75.8 17.4 %copy.17 = f32[256,128,128]{2,1,0:T(8,128)} copy(f32[256,128,128]{1,2,0:T(8,128)} %multiply_bitcast_fusion.1) | data formatting | bytes 33554432 | tf_op jit(solution)/shard_map/mul | solution.py:25
  93.2 0.2 broadcast_in_dim.22
  93.5 0.0 copy-start.3
  93.5 33.2 %scatter_fusion = f32[32,128,128]{2,1,0:T(8,128)S(1)} fusion(f32[32,128,128]{2,1,0:T(8,128)S(1)} %broadcast_in_dim.22, s32[256]{0:T(256)S(1)} %bitcast.43, f32[256,128,128]{2,1,0:T(8,128)} %copy.17), kind=kCustom, calls=%fused_computation.2 | custom fusion | flops 4194304 | bytes 50332672 | tf_op jit(solution)/shard_map/scatter-add | solution.py:27
  126.7 1.1 convert_element_type.38
  127.8 0.0 reduce-scatter.6.cloned.1.call-update
  127.8 0.0 reduce-scatter.10.cloned.1.call-start
  127.9 74.5 %reduce-scatter.6.cloned.1.call-done = bf16[512,128]{1,0:T(8,128)(2,1)} async-done(((bf16[4096,128]{1,0:T(8,128)(2,1)}), bf16[512,128]{1,0:T(8,128)(2,1)}) %reduce-scatter.6.cloned.1.call-update) | async-done | bytes 131088 | tf_op jit(solution)/shard_map/reduce_scatter | solution.py:29
  202.3 0.0 copy-done
  202.4 1.1 convolution_convert_fusion
  203.5 0.8 copy.22
  204.3 0.0 reduce-scatter.10.cloned.1.call-update
  204.3 0.0 all-gather.5.cloned.1.call-start
  204.4 16.0 %reduce-scatter.10.cloned.1.call-done = bf16[128,512]{1,0:T(8,128)(2,1)} async-done(((bf16[256,512]{1,0:T(8,128)(2,1)}), bf16[128,512]{1,0:T(8,128)(2,1)}) %reduce-scatter.10.cloned.1.call-update) | async-done | bytes 131088
  220.4 1.0 copy.23
  221.4 0.0 copy-done.3
  221.5 0.8 fusion.7
  222.3 5.9 all_gather.10
  228.2 0.9 convolution_convert_fusion.1
  229.0 0.0 all-gather.5.cloned.1.call-update
  229.1 0.0 all-reduce.2.cloned.1.call-start
  229.2 1.1 fusion.2
  230.3 0.0 copy-start.2
  230.3 0.7 copy-done.2
  231.0 0.0 all-reduce.2.cloned.1.call-update
  231.0 0.2 reduce-scatter.8.cloned.1.call-start
  231.3 50.6 %all-gather.5.cloned.1.call-done = bf16[4096,128]{1,0:T(8,128)(2,1)} async-done(((bf16[512,128]{1,0:T(8,128)(2,1)}), bf16[4096,128]{1,0:T(8,128)(2,1)}) %all-gather.5.cloned.1.call-update) | async-done | bytes 1048592 | tf_op jit(solution)/shard_map/all_gather | solution.py:58
  281.9 9.8 %gather_fusion.1 = bf16[256,128,128]{2,1,0:T(8,128)(2,1)} fusion(bf16[32,128,128]{2,1,0:T(8,128)(2,1)} %bitcast.35, s32[1024]{0:T(1024)S(1)} %pad_clamp_fusion), kind=kCustom, calls=%fused_computation.1 | custom fusion | bytes 16778240 | tf_op jit(solution)/shard_map/gather | solution.py:59
  291.7 15.4 %multiply_bitcast_fusion = f32[256,128,128]{1,2,0:T(8,128)} fusion(bf16[256,128,128]{2,1,0:T(8,128)(2,1)} %gather_fusion.1, bf16[1,1,256,128,128]{4,3,2,1,0:T(8,128)(2,1)} %param.11, f32[256]{0:T(256)S(1)} %compare_convert_fusion), kind=kOutput, calls=%fused_computation.4 | convolution fusion | flops 1077936128 | bytes 33555456 | tf_op jit(solution)/shard_map/tji,tjf->tif/dot_general | solution.py:60
  307.1 17.5 %copy.19 = f32[256,128,128]{2,1,0:T(8,128)} copy(f32[256,128,128]{1,2,0:T(8,128)} %multiply_bitcast_fusion) | data formatting | bytes 33554432 | tf_op jit(solution)/shard_map/mul | solution.py:63
  324.6 2.5 broadcast_in_dim.23
  327.0 0.0 copy-start.1
  327.0 52.1 %scatter_fusion.1 = f32[64,128,128]{2,1,0:T(8,128)} fusion(f32[64,128,128]{2,1,0:T(8,128)} %broadcast_in_dim.23, s32[256]{0:T(256)S(1)} %bitcast.42, f32[256,128,128]{2,1,0:T(8,128)} %copy.19), kind=kCustom, calls=%fused_computation.3 | custom fusion | flops 4194304 | bytes 50332672 | tf_op jit(solution)/shard_map/scatter-add | solution.py:65
  379.1 3.9 convert_element_type.46
  383.0 0.0 reduce-scatter.8.cloned.1.call-update
  383.1 154.2 %all-reduce.2.cloned.1.call-done = f32[2,128,256]{2,1,0:T(8,128)} async-done(((f32[2,128,256]{2,1,0:T(8,128)}), f32[2,128,256]{2,1,0:T(8,128)}) %all-reduce.2.cloned.1.call-update) | async-done | bytes 262160 | tf_op jit(solution)/shard_map/psum | solution.py:51
  537.3 1.6 multiply_bitcast_fusion.2
  538.8 59.4 %reduce-scatter.8.cloned.1.call-done = bf16[512,128]{1,0:T(8,128)(2,1)} async-done(((bf16[8192,128]{1,0:T(8,128)(2,1)}), bf16[512,128]{1,0:T(8,128)(2,1)}) %reduce-scatter.8.cloned.1.call-update) | async-done | bytes 131088 | tf_op jit(solution)/shard_map/reduce_scatter | solution.py:67
  598.3 0.0 copy-done.1
  (4 shorter events, 0.0 us)
Async XLA Ops:
  7.2 195.2 %copy-start = (bf16[256,256]{1,0:T(8,128)(2,1)S(1)}, bf16[256,256]{1,0:T(8,128)(2,1)}, u32[]{:S(2)}) copy-start(bf16[256,256]{1,0:T(8,128)(2,1)} %param.12) | copy-start | bytes 393220
  7.2 45.4 %all-gather.3.cloned.1.call-start = ((), (), s32[]{:S(2)}) async-start(), calls=%async_computation.3 | async-start | bytes 2228224 | tf_op jit(solution)/shard_map/all_gather | solution.py:22
  7.9 194.4 %reduce-scatter.6.cloned.1.call-start = ((), (), s32[]{:S(2)}) async-start(), calls=%async_computation.4 | async-start | bytes 1179648 | tf_op jit(solution)/shard_map/reduce_scatter | solution.py:29
  93.5 128.0 %copy-start.3 = (bf16[512,128]{1,0:T(8,128)(2,1)S(1)}, bf16[512,128]{1,0:T(8,128)(2,1)}, u32[]{:S(2)}) copy-start(bf16[512,128]{1,0:T(8,128)(2,1)} %param.13) | copy-start | bytes 393220
  127.8 92.6 %reduce-scatter.10.cloned.1.call-start = ((), (), s32[]{:S(2)}) async-start(), calls=%async_computation.8 | async-start | bytes 393216
  204.3 77.5 %all-gather.5.cloned.1.call-start = ((), (), s32[]{:S(2)}) async-start(), calls=%async_computation.5 | async-start | bytes 1179648 | tf_op jit(solution)/shard_map/all_gather | solution.py:58
  229.1 308.2 %all-reduce.2.cloned.1.call-start = ((), (), s32[]{:S(2)}) async-start(), calls=%async_computation.7 | async-start | bytes 524288 | tf_op jit(solution)/shard_map/psum | solution.py:51
  230.3 0.7 copy-start.2
  231.0 367.2 %reduce-scatter.8.cloned.1.call-start = ((), (), s32[]{:S(2)}) async-start(), calls=%async_computation.6 | async-start | bytes 2228224 | tf_op jit(solution)/shard_map/reduce_scatter | solution.py:67
  327.0 271.2 %copy-start.1 = (bf16[256,256]{1,0:T(8,128)(2,1)S(1)}, bf16[256,256]{1,0:T(8,128)(2,1)}, u32[]{:S(2)}) copy-start(bf16[256,256]{1,0:T(8,128)(2,1)} %param.12) | copy-start | bytes 393220
Sparse Core Ops, SparseCore 0:
  9.8 42.6 all-gather.2
  127.9 74.3 reduce-scatter.5
  205.0 15.3 reduce-scatter.9
  229.2 52.6 all-gather.4
  287.2 250.0 all-reduce.1
  540.2 57.9 reduce-scatter.7
where the time goes:
time: 607 us; the launch traced here: 605 us
  waiting for transfers between devices  399 us (66%)
  other arithmetic  93.4 us (15%)
  local copies, waits for them, and re-layouts  60.2 us (10%)
  matrix products  31.5 us (5%)
  between operations  14.9 us (2%)
    psum x1, waiting for transfers between devices, shards(): slots = lax.psum(slots, ('row', 'col', 'feat'))  154 us
    reduce_scatter x1, waiting for transfers between devices, shards(): lax.psum_scatter(partial_value.reshape(row_blocks * width, feat_half).ast...  74.5 us
    reduce_scatter x1, waiting for transfers between devices, shards(): lax.psum_scatter(back_partial.reshape(col_blocks * width, feat_half).asty...  59.4 us
    scatter-add x1, other arithmetic, shards(): jnp.zeros((col_blocks, width, feat_half), jnp.float32).at[block_cols]  52.1 us
    all_gather x1, waiting for transfers between devices, shards(): spread_panel = lax.all_gather(spread, 'col', axis=0, tiled=True)  50.6 us
    all_gather x1, waiting for transfers between devices, shards(): panel = lax.all_gather(features, 'row', axis=0, tiled=True)  43.2 us
    scatter-add x1, other arithmetic, shards(): jnp.zeros((row_blocks, width, feat_half), jnp.float32).at[block_rows]  33.2 us
    mul x1, local copies, waits for them, and re-layouts, shards(): back_products = back_products * live_mask[:, None, None]  17.5 us
  transfers between devices with their start and end apart: 6, of which 6 were waited for; matrix products, arithmetic and copies ran while one was open for 17% of the time, Pallas kernels for 0%

commit v1 on v0

--- a/solution.py
+++ b/solution.py
@@ -48,7 +48,7 @@
     n_feat = lax.axis_size("feat")
     slots = jnp.zeros((n_feat,) + weight_term.shape, jnp.float32)
     slots = lax.dynamic_update_slice_in_dim(slots, weight_term[None], feat_index, 0)
-    slots = lax.psum(slots, ("row", "col", "feat"))
+    slots = lax.psum(lax.psum(slots, "row"), ("col", "feat"))
     weight_grad = lax.dynamic_index_in_dim(slots, feat_index, 0, keepdims=False) * node_total ** (
         -0.5
     )

time: 607 us -> 564 us (0.929)
  waiting for transfers between devices: 399 us -> 356 us
    psum x1 -> x2, waiting for transfers between devices: 154 us -> 110 us  [shards(): slots = lax.psum(lax.psum(slots, 'row'), ('col', 'feat'))]
    unnamed x7 -> x8, waiting for transfers between devices: 16.8 us -> 16.8 us
  transfers between devices with their start and end apart: 6 -> 7, of which waited for: 6 -> 6; matrix products, arithmetic and copies ran while one was open for 17% -> 19% of each run, Pallas kernels for 0% -> 0%
where the time goes in v1:
time: 564 us; the launch traced here: 562 us
  waiting for transfers between devices  356 us (63%)
  other arithmetic  93.4 us (17%)
  local copies, waits for them, and re-layouts  60.2 us (11%)
  matrix products  31.6 us (6%)
  between operations  14.9 us (3%)
  blocking collectives  5.89 us (1%)
    psum x2, waiting for transfers between devices, shards(): slots = lax.psum(lax.psum(slots, 'row'), ('col', 'feat'))  110 us
    reduce_scatter x1, waiting for transfers between devices, shards(): lax.psum_scatter(partial_value.reshape(row_blocks * width, feat_half).ast...  74.5 us
    reduce_scatter x1, waiting for transfers between devices, shards(): lax.psum_scatter(back_partial.reshape(col_blocks * width, feat_half).asty...  57.5 us
    all_gather x1, waiting for transfers between devices, shards(): spread_panel = lax.all_gather(spread, 'col', axis=0, tiled=True)  54.1 us
    scatter-add x1, other arithmetic, shards(): jnp.zeros((col_blocks, width, feat_half), jnp.float32).at[block_cols]  52 us
    all_gather x1, waiting for transfers between devices, shards(): panel = lax.all_gather(features, 'row', axis=0, tiled=True)  43.2 us
    scatter-add x1, other arithmetic, shards(): jnp.zeros((row_blocks, width, feat_half), jnp.float32).at[block_rows]  33.2 us
    mul x1, local copies, waits for them, and re-layouts, shards(): back_products = back_products * live_mask[:, None, None]  17.5 us
  transfers between devices with their start and end apart: 7, of which 6 were waited for; matrix products, arithmetic and copies ran while one was open for 19% of the time, Pallas kernels for 0%

profile of v1, /device:TPU:2, one launch (start us, length us, event | category | flops | bytes accessed | tf_op | source)
XLA Modules:
  0.0 562.3 jit_solution(4279256555704040123)
XLA Ops:
  7.2 0.0 copy-start
  7.2 0.0 all-gather.3.cloned.1.call-start
  7.2 0.7 all-gather.3.cloned.1.call-update
  7.9 0.0 reduce-scatter.6.cloned.1.call-start
  8.6 0.7 compare_select_fusion
  9.3 43.2 %all-gather.3.cloned.1.call-done = bf16[8192,128]{1,0:T(8,128)(2,1)} async-done(((bf16[512,128]{1,0:T(8,128)(2,1)}), bf16[8192,128]{1,0:T(8,128)(2,1)}) %all-gather.3.cloned.1.call-update) | async-done | bytes 2097168 | tf_op jit(solution)/shard_map/all_gather | solution.py:22
  52.6 10.2 %gather_fusion = bf16[256,128,128]{2,1,0:T(8,128)(2,1)} fusion(bf16[64,128,128]{2,1,0:T(8,128)(2,1)} %bitcast.36, s32[1024]{0:T(1024)S(1)} %pad_clamp_fusion.1), kind=kCustom, calls=%fused_computation | custom fusion | bytes 16778240 | tf_op jit(solution)/shard_map/gather | solution.py:23
  62.8 13.0 %multiply_bitcast_fusion.1 = f32[256,128,128]{1,2,0:T(8,128)} fusion(bf16[256,128,128]{2,1,0:T(8,128)(2,1)} %gather_fusion, bf16[1,1,256,128,128]{4,3,2,1,0:T(8,128)(2,1)} %param.11, f32[256]{0:T(256)S(1)} %compare_convert_fusion), kind=kOutput, calls=%fused_computation.5 | convolution fusion | flops 1077936128 | bytes 33555456 | tf_op jit(solution)/shard_map/tij,tjf->tif/dot_general | solution.py:24
  75.8 17.4 %copy.17 = f32[256,128,128]{2,1,0:T(8,128)} copy(f32[256,128,128]{1,2,0:T(8,128)} %multiply_bitcast_fusion.1) | data formatting | bytes 33554432 | tf_op jit(solution)/shard_map/mul | solution.py:25
  93.2 0.2 broadcast_in_dim.22
  93.5 0.0 copy-start.3
  93.5 33.2 %scatter_fusion = f32[32,128,128]{2,1,0:T(8,128)S(1)} fusion(f32[32,128,128]{2,1,0:T(8,128)S(1)} %broadcast_in_dim.22, s32[256]{0:T(256)S(1)} %bitcast.43, f32[256,128,128]{2,1,0:T(8,128)} %copy.17), kind=kCustom, calls=%fused_computation.2 | custom fusion | flops 4194304 | bytes 50332672 | tf_op jit(solution)/shard_map/scatter-add | solution.py:27
  126.7 1.1 convert_element_type.38
  127.8 0.0 reduce-scatter.6.cloned.1.call-update
  127.8 0.0 reduce-scatter.10.cloned.1.call-start
  127.9 74.5 %reduce-scatter.6.cloned.1.call-done = bf16[512,128]{1,0:T(8,128)(2,1)} async-done(((bf16[4096,128]{1,0:T(8,128)(2,1)}), bf16[512,128]{1,0:T(8,128)(2,1)}) %reduce-scatter.6.cloned.1.call-update) | async-done | bytes 131088 | tf_op jit(solution)/shard_map/reduce_scatter | solution.py:29
  202.3 0.0 copy-done
  202.4 1.1 convolution_convert_fusion
  203.5 0.8 copy.22
  204.3 0.0 reduce-scatter.10.cloned.1.call-update
  204.3 0.0 all-reduce.3.cloned.1.call-start
  204.4 16.0 %reduce-scatter.10.cloned.1.call-done = bf16[128,512]{1,0:T(8,128)(2,1)} async-done(((bf16[256,512]{1,0:T(8,128)(2,1)}), bf16[128,512]{1,0:T(8,128)(2,1)}) %reduce-scatter.10.cloned.1.call-update) | async-done | bytes 131088
  220.4 1.0 copy.23
  221.4 0.0 copy-done.3
  221.5 0.8 fusion.7
  222.3 5.9 %all_gather.10 = bf16[512,256]{1,0:T(8,128)(2,1)S(1)} all-gather(bf16[512,128]{1,0:T(8,128)(2,1)S(1)} %get-tuple-element.3), channel_id=1, replica_groups=mesh['row'=16,'col'=8,'feat'=2] {'feat'}, dimensions={1}, use_global_device_ids=true | all-gather | bytes 393216 | tf_op jit(solution)/shard_map/all_gather | solution.py:44
  228.2 1.1 fusion.2
  229.3 0.0 copy-start.2
  229.3 0.7 copy-done.2
  230.0 0.0 all-reduce.3.cloned.1.call-update
  230.0 0.0 all-gather.5.cloned.1.call-start
  230.1 0.9 convolution_convert_fusion.1
  231.0 0.0 all-gather.5.cloned.1.call-update
  231.0 0.0 all-reduce.5.cloned.1.call-start
  231.1 109.8 %all-reduce.3.cloned.1.call-done = f32[2,128,256]{2,1,0:T(8,128)} async-done(((f32[2,128,256]{2,1,0:T(8,128)}), f32[2,128,256]{2,1,0:T(8,128)}) %all-reduce.3.cloned.1.call-update) | async-done | bytes 262160 | tf_op jit(solution)/shard_map/psum | solution.py:51
  340.9 0.0 all-reduce.5.cloned.1.call-update
  340.9 0.2 reduce-scatter.8.cloned.1.call-start
  341.1 54.1 %all-gather.5.cloned.1.call-done = bf16[4096,128]{1,0:T(8,128)(2,1)} async-done(((bf16[512,128]{1,0:T(8,128)(2,1)}), bf16[4096,128]{1,0:T(8,128)(2,1)}) %all-gather.5.cloned.1.call-update) | async-done | bytes 1048592 | tf_op jit(solution)/shard_map/all_gather | solution.py:58
  395.2 9.8 %gather_fusion.1 = bf16[256,128,128]{2,1,0:T(8,128)(2,1)} fusion(bf16[32,128,128]{2,1,0:T(8,128)(2,1)} %bitcast.35, s32[1024]{0:T(1024)S(1)} %pad_clamp_fusion), kind=kCustom, calls=%fused_computation.1 | custom fusion | bytes 16778240 | tf_op jit(solution)/shard_map/gather | solution.py:59
  405.0 15.5 %multiply_bitcast_fusion = f32[256,128,128]{1,2,0:T(8,128)} fusion(bf16[256,128,128]{2,1,0:T(8,128)(2,1)} %gather_fusion.1, bf16[1,1,256,128,128]{4,3,2,1,0:T(8,128)(2,1)} %param.11, f32[256]{0:T(256)S(1)} %compare_convert_fusion), kind=kOutput, calls=%fused_computation.4 | convolution fusion | flops 1077936128 | bytes 33555456 | tf_op jit(solution)/shard_map/tji,tjf->tif/dot_general | solution.py:60
  420.5 17.5 %copy.19 = f32[256,128,128]{2,1,0:T(8,128)} copy(f32[256,128,128]{1,2,0:T(8,128)} %multiply_bitcast_fusion) | data formatting | bytes 33554432 | tf_op jit(solution)/shard_map/mul | solution.py:63
  437.9 2.5 broadcast_in_dim.23
  440.4 0.0 copy-start.1
  440.4 52.0 %scatter_fusion.1 = f32[64,128,128]{2,1,0:T(8,128)} fusion(f32[64,128,128]{2,1,0:T(8,128)} %broadcast_in_dim.23, s32[256]{0:T(256)S(1)} %bitcast.42, f32[256,128,128]{2,1,0:T(8,128)} %copy.19), kind=kCustom, calls=%fused_computation.3 | custom fusion | flops 4194304 | bytes 50332672 | tf_op jit(solution)/shard_map/scatter-add | solution.py:65
  492.4 3.9 convert_element_type.46
  496.4 0.0 reduce-scatter.8.cloned.1.call-update
  496.4 0.0 all-reduce.5.cloned.1.call-done
  496.4 1.6 multiply_bitcast_fusion.2
  498.0 57.5 %reduce-scatter.8.cloned.1.call-done = bf16[512,128]{1,0:T(8,128)(2,1)} async-done(((bf16[8192,128]{1,0:T(8,128)(2,1)}), bf16[512,128]{1,0:T(8,128)(2,1)}) %reduce-scatter.8.cloned.1.call-update) | async-done | bytes 131088 | tf_op jit(solution)/shard_map/reduce_scatter | solution.py:67
  555.4 0.0 copy-done.1
  (4 shorter events, 0.0 us)
Async XLA Ops:
  7.2 195.2 %copy-start = (bf16[256,256]{1,0:T(8,128)(2,1)S(1)}, bf16[256,256]{1,0:T(8,128)(2,1)}, u32[]{:S(2)}) copy-start(bf16[256,256]{1,0:T(8,128)(2,1)} %param.12) | copy-start | bytes 393220
  7.2 45.4 %all-gather.3.cloned.1.call-start = ((), (), s32[]{:S(2)}) async-start(), calls=%async_computation.3 | async-start | bytes 2228224 | tf_op jit(solution)/shard_map/all_gather | solution.py:22
  7.9 194.4 %reduce-scatter.6.cloned.1.call-start = ((), (), s32[]{:S(2)}) async-start(), calls=%async_computation.4 | async-start | bytes 1179648 | tf_op jit(solution)/shard_map/reduce_scatter | solution.py:29
  93.5 128.0 %copy-start.3 = (bf16[512,128]{1,0:T(8,128)(2,1)S(1)}, bf16[512,128]{1,0:T(8,128)(2,1)}, u32[]{:S(2)}) copy-start(bf16[512,128]{1,0:T(8,128)(2,1)} %param.13) | copy-start | bytes 393220
  127.8 92.6 %reduce-scatter.10.cloned.1.call-start = ((), (), s32[]{:S(2)}) async-start(), calls=%async_computation.9 | async-start | bytes 393216
  204.3 136.5 %all-reduce.3.cloned.1.call-start = ((), (), s32[]{:S(2)}) async-start(), calls=%async_computation.7 | async-start | bytes 524288 | tf_op jit(solution)/shard_map/psum | solution.py:51
  229.3 0.7 copy-start.2
  230.0 165.2 %all-gather.5.cloned.1.call-start = ((), (), s32[]{:S(2)}) async-start(), calls=%async_computation.5 | async-start | bytes 1179648 | tf_op jit(solution)/shard_map/all_gather | solution.py:58
  231.0 265.4 %all-reduce.5.cloned.1.call-start = ((), (), s32[]{:S(2)}) async-start(), calls=%async_computation.8 | async-start | bytes 524288 | tf_op jit(solution)/shard_map/psum | solution.py:51
  340.9 214.5 %reduce-scatter.8.cloned.1.call-start = ((), (), s32[]{:S(2)}) async-start(), calls=%async_computation.6 | async-start | bytes 2228224 | tf_op jit(solution)/shard_map/reduce_scatter | solution.py:67
  440.4 115.0 %copy-start.1 = (bf16[256,256]{1,0:T(8,128)(2,1)S(1)}, bf16[256,256]{1,0:T(8,128)(2,1)}, u32[]{:S(2)}) copy-start(bf16[256,256]{1,0:T(8,128)(2,1)} %param.12) | copy-start | bytes 393220
Sparse Core Ops, SparseCore 0:
  9.8 42.6 all-gather.2
  127.9 74.3 reduce-scatter.5
  205.0 15.3 reduce-scatter.9
  230.2 110.6 all-reduce.2
  344.3 50.8 all-gather.4
  398.5 93.7 all-reduce.4
  496.5 58.8 reduce-scatter.7
